TPU v7x, 32 devices: a whole 2x2x4 slice. The times are simulated.
32 devices in a mesh: shard: 8 (over y, x, core), tensor: 4 (over z).
Axes of the slice: x: 2, y: 2, z: 4, core: 2. Of those that a mesh axis runs over, the one named last changes fastest.
Arguments:
- step: int32 [1], replicated, may hold values from 1 to 19
- lengths: int32 [80], replicated, may hold values from 1 to 262144, 2097152 in all
- grads: bfloat16 [8, 8, 4, 65536], P('shard', None, 'tensor'), may hold values from -2 to 2
- weights: float32 [2097152], P(('shard', 'tensor'))
- moment1: float32 [2097152], P(('shard', 'tensor')), may hold values from -0.4375 to 0.4375
- moment2: float32 [2097152], P(('shard', 'tensor')), may hold values from 0.0001 to 0.01
Outputs:
- new_weights: float32 [2097152], P(('shard', 'tensor'))
- new_moment1: float32 [2097152], P(('shard', 'tensor'))
- new_moment2: float32 [2097152], P(('shard', 'tensor'))
- train_weights: bfloat16 [8, 4, 65536], P(None, 'tensor')
Inputs may be any that keep to these rules, and one draw needn't show every extreme that they name: The lengths sum to 2097152, and one of them equals 262144.
All inputs are finite; a program needn't handle non-finite values.
Results may differ from a plain program's by a relative error of at most 0.0004.
Values may be sent and summed in bfloat16 or wider, within the bound.
No kernel may reach another device: no remote copies, remote signals or barrier semaphores. Data moves between devices by JAX's collectives and lax.ppermute only.
A program may use at most 128 MiB of HBM per device.

v0:
```python
import math
import jax
import jax.numpy as jnp
from jax import lax
from jax.sharding import PartitionSpec as P


def segment_squares(columns, base, starts, ends):
    width = columns.shape[1]
    block = math.gcd(width, 8192)
    blocks = width // block
    pieces = columns.reshape(columns.shape[0], blocks, block).transpose(1, 0, 2)
    places = base + jnp.arange(width, dtype=jnp.int32).reshape(blocks, block)

    def add_block(total, item):
        piece, place = item
        member = ((place[None, :] >= starts[:, None]) & (place[None, :] < ends[:, None])).astype(
            jnp.float32
        )
        return (total + jnp.dot(member, piece.T, precision=lax.Precision.HIGHEST), None)

    init = jnp.zeros((starts.shape[0], columns.shape[0]), jnp.float32)
    total, unused = lax.scan(add_block, init, (pieces, places))
    return total


def spread_ratio(ratio, base, starts, ends, width):
    block = math.gcd(width, 8192)
    blocks = width // block
    places = base + jnp.arange(width, dtype=jnp.int32).reshape(blocks, block)

    def expand(carry, place):
        member = ((place[None, :] >= starts[:, None]) & (place[None, :] < ends[:, None])).astype(
            jnp.float32
        )
        return (carry, jnp.dot(ratio[None, :], member, precision=lax.Precision.HIGHEST)[0])

    unused, rows = lax.scan(expand, jnp.float32(0.0), places)
    return rows.reshape(width)


def local(step, lengths, grads, weights, moment1, moment2):
    width = weights.shape[0]
    base = (lax.axis_index("shard") * lax.axis_size("tensor") + lax.axis_index("tensor")) * width
    ends = jnp.cumsum(lengths)
    starts = ends - lengths
    flat_grads = grads.reshape(-1)
    grad = lax.psum_scatter(
        flat_grads.astype(jnp.float32), "shard", scatter_dimension=0, tiled=True
    )
    count = step[0].astype(jnp.float32)
    first = 1.0 - jnp.power(jnp.float32(0.9), count)
    second = 1.0 - jnp.power(jnp.float32(0.999), count)
    new_moment1 = 0.9 * moment1 + 0.1 * grad
    new_moment2 = 0.999 * moment2 + 0.001 * grad * grad
    update = new_moment1 / first / (jnp.sqrt(new_moment2 / second) + 1e-06) + 0.1 * weights
    stacked = jnp.stack([weights * weights, update * update])
    partial_value = segment_squares(stacked, base, starts, ends)
    wsq, usq = lax.psum((partial_value[:, 0], partial_value[:, 1]), ("shard", "tensor"))
    ratio = jnp.sqrt(wsq) / jnp.maximum(jnp.sqrt(usq), 1.0)
    local_ratio = spread_ratio(ratio, base, starts, ends, width)
    new_weights = weights - 0.25 * local_ratio * update
    rounded = new_weights.astype(jnp.bfloat16).reshape(1, 1, width)
    train_weights = lax.all_gather(rounded, "shard", axis=0, tiled=True)
    return (new_weights, new_moment1, new_moment2, train_weights)


def solution(mesh):
    placed = (
        P(),
        P(),
        P("shard", None, "tensor", None),
        P(("shard", "tensor")),
        P(("shard", "tensor")),
        P(("shard", "tensor")),
    )
    return jax.shard_map(
        local,
        mesh=mesh,
        in_specs=placed,
        out_specs=(
            P(("shard", "tensor")),
            P(("shard", "tensor")),
            P(("shard", "tensor")),
            P(None, "tensor", None),
        ),
        check_vma=False,
    )
```

profile of v0, /device:TPU:0, one launch (start us, length us, event | category | flops | bytes accessed | tf_op | source)
XLA Modules:
  0.0 172.9 jit_solution(6423546391148193087)
XLA Ops:
  7.2 1.4 convert_bitcast_fusion
  8.6 1.7 copy.13
  11.6 0.6 dynamic-slice
  12.9 62.5 %all-reduce.4.cloned.1.call-done = f32[524288]{0:T(1024)} async-done(((f32[524288]{0:T(1024)}), f32[524288]{0:T(1024)}) %all-reduce.4.cloned.1.call-update) | async-done | bytes 2097168
  75.4 1.2 fusion.14
  76.6 0.5 maximum_bitcast_fusion
  77.0 12.3 %while.22 = (s32[]{:T(128)}, f32[80,2]{0,1:T(2,128)S(1)}, s32[8,8192]{1,0:T(8,128)S(1)}, s32[80]{0:T(128)S(1)}, s32[80]{0:T(128)S(1)}, /*index=5*/f32[8,2,8192]{2,1,0:T(2,128)S(1)}, s32[]{:T(128)}, s32[]{:T(128)}) while((s32[]{:T(128)}, f32[80,2]{0,1:T(2,128)S(1)}, s32[8,8192]{1,0:T(8,128)S(1)}, s32[80]{0:T(128)S(1)}, ...), condition=%wide.region_3.4_spmd.clone, body=%wide.region_2.3_spmd.clone.sunk | while | flops 17695044 | bytes 166631 | solution.py:23
  77.1 1.5 fusion.24
  78.6 1.5 fusion.24
  80.2 1.5 fusion.24
  81.7 1.5 fusion.24
  83.2 1.5 fusion.24
  84.8 1.5 fusion.24
  86.3 1.5 fusion.24
  87.9 1.5 fusion.24
  89.4 39.4 %all-reduce.1 = (f32[80]{0:T(128)S(1)}, f32[80]{0:T(128)S(1)}) all-reduce(f32[80]{0:T(128)S(1)} %get-tuple-element.124, f32[80]{0:T(128)S(1)} %get-tuple-element.123), channel_id=1, replica_groups=mesh['shard'=8,'tensor'=4] {'shard','tensor'}, use_global_device_ids=true, to_apply=%region_5.6 | all-reduce | flops 160 | bytes 1280 | tf_op jit(solution)/shard_map/psum | solution.py:59
  128.7 10.2 %while.21 = (s32[]{:T(128)}, f32[8,8192]{1,0:T(8,128)S(1)}, s32[8,8192]{1,0:T(8,128)S(1)}, s32[80]{0:T(128)S(1)}, s32[80]{0:T(128)S(1)}, /*index=5*/f32[80]{0:T(128)S(1)}, s32[]{:T(128)}, s32[]{:T(128)}) while((s32[]{:T(128)}, f32[8,8192]{1,0:T(8,128)S(1)}, s32[8,8192]{1,0:T(8,128)S(1)}, s32[80]{0:T(128)S(1)}, s32[80]{0:T(128)S(1)}, ...), condition=%wide.region_7.8_spmd, body=%wide.region_6.7_spmd.sunk | while | flops 9830402 | bytes 197661 | solution.py:38
  128.8 1.1 fusion.22
  129.9 0.1 dynamic_update_slice.5
  130.1 1.1 fusion.22
  131.1 0.1 dynamic_update_slice.5
  131.3 1.1 fusion.22
  132.4 0.1 dynamic_update_slice.5
  132.6 1.1 fusion.22
  133.7 0.1 dynamic_update_slice.5
  133.9 1.1 fusion.22
  135.1 1.1 fusion.22
  136.4 1.1 fusion.22
  137.7 1.1 fusion.22
  139.0 0.9 fusion.15
  140.0 23.5 %all-gather.3.cloned.1.call-done = bf16[524288]{0:T(1024)(128)(2,1)} async-done(((bf16[65536]{0:T(1024)(128)(2,1)}), bf16[524288]{0:T(1024)(128)(2,1)}) %all-gather.3.cloned.1.call-update) | async-done | bytes 1048592 | tf_op jit(solution)/shard_map/all_gather | solution.py:64
  163.5 2.6 %reshape.79 = bf16[8,1,65536]{2,0,1:T(8,128)(2,1)} reshape(bf16[524288]{0:T(1024)(128)(2,1)} %all-gather.3.cloned.1.call-done) | data formatting | bytes 2097152 | tf_op jit(solution)/shard_map/all_gather | solution.py:64
  (49 shorter events, 1.6 us)
Async XLA Ops:
  7.2 68.2 %all-reduce.4.cloned.1.call-start = ((), (), s32[]{:S(2)}) async-start(), calls=%async_computation.1 | async-start | bytes 4194304
  10.3 0.9 copy-start.5
  10.3 1.3 copy-start.6
  10.3 65.1 %copy-start = (f32[65536]{0:T(1024)S(1)}, f32[65536]{0:T(1024)}, u32[]{:S(2)}) copy-start(f32[65536]{0:T(1024)} %param.13) | copy-start | bytes 786436
  10.3 65.1 %copy-start.3 = (f32[65536]{0:T(1024)S(1)}, f32[65536]{0:T(1024)}, u32[]{:S(2)}) copy-start(f32[65536]{0:T(1024)} %param.15) | copy-start | bytes 786436
  10.3 65.1 %copy-start.4 = (f32[65536]{0:T(1024)S(1)}, f32[65536]{0:T(1024)}, u32[]{:S(2)}) copy-start(f32[65536]{0:T(1024)} %param.14) | copy-start | bytes 786436
  10.3 153.2 %all-gather.3.cloned.1.call-start = ((), (), s32[]{:S(2)}) async-start(), calls=%async_computation | async-start | bytes 1179648 | tf_op jit(solution)/shard_map/all_gather | solution.py:64
  76.5 62.5 %copy-start.1 = (f32[65536]{0:T(1024)}, f32[65536]{0:T(1024)S(1)}, u32[]{:S(2)}) copy-start(f32[65536]{0:T(1024)S(1)} %get-tuple-element.120) | copy-start | bytes 786436
  76.6 62.5 %copy-start.2 = (f32[65536]{0:T(1024)}, f32[65536]{0:T(1024)S(1)}, u32[]{:S(2)}) copy-start(f32[65536]{0:T(1024)S(1)} %get-tuple-element.121) | copy-start | bytes 786436
Sparse Core Ops, SparseCore 0:
  11.2 64.0 all-reduce.3
  140.1 23.3 all-gather.2
where the time goes:
time: 173 us
  waiting for transfers between devices  86.1 us (50%)
  blocking collectives  39.4 us (23%)
  matrix products  20.4 us (12%)
  between operations  15.7 us (9%)
  local copies, waits for them, and re-layouts  6.7 us (4%)
  other arithmetic  4.19 us (2%)
    unnamed x3, waiting for transfers between devices  62.5 us
    psum x1, blocking collectives, local(): lax.psum((partial_value[:, 0], partial_value[:, 1]), ('shard', 'tensor'))  39.4 us
    all_gather x1, waiting for transfers between devices, local(): train_weights = lax.all_gather(rounded, 'shard', axis=0, tiled=True)  23.5 us
    dot_general x8, matrix products, add_block(): jnp.dot(member, piece.T, precision=lax.Precision.HIGHEST)  11.8 us
    dot_general x8, matrix products, expand(): jnp.dot(ratio[None, :], member, precision=lax.Precision.HIGHEST)[0]  8.56 us
  transfers between devices with their start and end apart: 2, of which 2 were waited for; matrix products, arithmetic and copies ran while one was open for 1% of the time, Pallas kernels for 0%

commit v1 on v0

--- a/solution.py
+++ b/solution.py
@@ -61,7 +61,23 @@
     local_ratio = spread_ratio(ratio, base, starts, ends, width)
     new_weights = weights - 0.25 * local_ratio * update
     rounded = new_weights.astype(jnp.bfloat16).reshape(1, 1, width)
-    train_weights = lax.all_gather(rounded, "shard", axis=0, tiled=True)
+    ways, here, step_2 = (lax.axis_size("shard"), lax.axis_index("shard"), rounded.shape[0])
+    shape = [n * ways if d == 0 else n for d, n in enumerate(rounded.shape)]
+    full = lax.dynamic_update_slice_in_dim(
+        jnp.zeros(shape, rounded.dtype), rounded, here * step_2, axis=0
+    )
+    going_up = going_down = rounded
+    for far in range(1, ways // 2 + 1):
+        going_up = lax.ppermute(going_up, "shard", [(d, (d + 1) % ways) for d in range(ways)])
+        full = lax.dynamic_update_slice_in_dim(full, going_up, (here - far) % ways * step_2, axis=0)
+        if 2 * far < ways:
+            going_down = lax.ppermute(
+                going_down, "shard", [(d, (d - 1) % ways) for d in range(ways)]
+            )
+            full = lax.dynamic_update_slice_in_dim(
+                full, going_down, (here + far) % ways * step_2, axis=0
+            )
+    train_weights = full
     return (new_weights, new_moment1, new_moment2, train_weights)
 
 

time: 173 us -> 211 us (1.22); the launches traced: 173 us -> 209 us
  local copies, waits for them, and re-layouts: 6.7 us -> 40.6 us
  starting transfers between devices: 0.08 us -> 8.23 us
  waiting for transfers between devices: 86.1 us -> 79.7 us
    dynamic_update_slice x0 -> x8, local copies, waits for them, and re-layouts: none -> 35.4 us  [the longest x4 17.7 us: local(): lax.dynamic_update_slice_in_dim(full, going_up, (here - far) % ways * ste...]
    all_gather x1 -> x0, waiting for transfers between devices: 23.5 us -> none  [local(): train_weights = lax.all_gather(rounded, 'shard', axis=0, tiled=True)]
    ppermute x0 -> x7, waiting for transfers between devices: none -> 17.1 us  [the longest x4 16.5 us: local(): lax.ppermute(going_up, 'shard', [(d, (d + 1) % ways) for d in range(ways)])]
    ppermute x0 -> x7, starting transfers between devices: none -> 8.19 us  [the longest x3 8.12 us: local(): lax.ppermute(going_down, 'shard', [(d, (d - 1) % ways) for d in range(way...]
    all_gather x1 -> x0, local copies, waits for them, and re-layouts: 2.64 us -> none  [local(): train_weights = lax.all_gather(rounded, 'shard', axis=0, tiled=True)]
    unnamed x3 -> x2, waiting for transfers between devices: 62.5 us -> 62.6 us
  transfers between devices with their start and end apart: 2 -> 8, of which waited for: 2 -> 5; matrix products, arithmetic and copies ran while one was open for 1% -> 15% of each run, Pallas kernels for 0% -> 0%
where the time goes in v1:
time: 211 us; the launch traced here: 209 us
  waiting for transfers between devices  79.7 us (38%)
  local copies, waits for them, and re-layouts  40.6 us (19%)
  blocking collectives  39.3 us (19%)
  matrix products  20.4 us (10%)
  between operations  15.8 us (7%)
  starting transfers between devices  8.23 us (4%)
  other arithmetic  4.14 us (2%)
    unnamed x2, waiting for transfers between devices  62.6 us
    psum x1, blocking collectives, local(): lax.psum((partial_value[:, 0], partial_value[:, 1]), ('shard', 'tensor'))  39.3 us
    dynamic_update_slice x4, local copies, waits for them, and re-layouts, local(): lax.dynamic_update_slice_in_dim(full, going_up, (here - far) % ways * ste...  17.7 us
    ppermute x4, waiting for transfers between devices, local(): lax.ppermute(going_up, 'shard', [(d, (d + 1) % ways) for d in range(ways)])  16.5 us
    dynamic_update_slice x3, local copies, waits for them, and re-layouts, local(): lax.dynamic_update_slice_in_dim(full, going_down, (here + far) % ways * s...  13.3 us
    dot_general x8, matrix products, add_block(): jnp.dot(member, piece.T, precision=lax.Precision.HIGHEST)  11.8 us
    dot_general x8, matrix products, expand(): jnp.dot(ratio[None, :], member, precision=lax.Precision.HIGHEST)[0]  8.56 us
    ppermute x3, starting transfers between devices, local(): lax.ppermute(going_down, 'shard', [(d, (d - 1) % ways) for d in range(way...  8.12 us
  transfers between devices with their start and end apart: 8, of which 5 were waited for; matrix products, arithmetic and copies ran while one was open for 15% of the time, Pallas kernels for 0%

profile of v1, /device:TPU:0, one launch (start us, length us, event | category | flops | bytes accessed | tf_op | source)
XLA Modules:
  0.0 208.7 jit_solution(12174275310416380953)
XLA Ops:
  7.2 1.4 convert_bitcast_fusion
  8.6 1.7 copy.13
  12.8 62.6 %all-reduce.4.cloned.1.call-done = f32[524288]{0:T(1024)} async-done(((f32[524288]{0:T(1024)}), f32[524288]{0:T(1024)}) %all-reduce.4.cloned.1.call-update) | async-done | bytes 2097168
  75.4 1.2 fusion.14
  77.1 12.3 %while.22 = (s32[]{:T(128)}, f32[80,2]{0,1:T(2,128)S(1)}, s32[8,8192]{1,0:T(8,128)S(1)}, s32[80]{0:T(128)S(1)}, s32[80]{0:T(128)S(1)}, /*index=5*/f32[8,2,8192]{2,1,0:T(2,128)S(1)}, s32[]{:T(128)}, s32[]{:T(128)}) while((s32[]{:T(128)}, f32[80,2]{0,1:T(2,128)S(1)}, s32[8,8192]{1,0:T(8,128)S(1)}, s32[80]{0:T(128)S(1)}, ...), condition=%wide.region_3.4_spmd.clone, body=%wide.region_2.3_spmd.clone.sunk | while | flops 17695044 | bytes 166631 | solution.py:23
  77.1 1.5 fusion.24
  78.7 1.5 fusion.24
  80.2 1.5 fusion.24
  81.8 1.5 fusion.24
  83.3 1.5 fusion.24
  84.8 1.5 fusion.24
  86.4 1.5 fusion.24
  87.9 1.5 fusion.24
  89.4 39.3 %all-reduce.1 = (f32[80]{0:T(128)S(1)}, f32[80]{0:T(128)S(1)}) all-reduce(f32[80]{0:T(128)S(1)} %get-tuple-element.124, f32[80]{0:T(128)S(1)} %get-tuple-element.123), channel_id=1, replica_groups=mesh['shard'=8,'tensor'=4] {'shard','tensor'}, use_global_device_ids=true, to_apply=%region_5.6 | all-reduce | flops 160 | bytes 1280 | tf_op jit(solution)/shard_map/psum | solution.py:59
  128.8 10.2 %while.21 = (s32[]{:T(128)}, f32[8,8192]{1,0:T(8,128)S(1)}, s32[8,8192]{1,0:T(8,128)S(1)}, s32[80]{0:T(128)S(1)}, s32[80]{0:T(128)S(1)}, /*index=5*/f32[80]{0:T(128)S(1)}, s32[]{:T(128)}, s32[]{:T(128)}) while((s32[]{:T(128)}, f32[8,8192]{1,0:T(8,128)S(1)}, s32[8,8192]{1,0:T(8,128)S(1)}, s32[80]{0:T(128)S(1)}, s32[80]{0:T(128)S(1)}, ...), condition=%wide.region_7.8_spmd, body=%wide.region_6.7_spmd.sunk | while | flops 9830402 | bytes 197661 | solution.py:38
  128.8 1.1 fusion.22
  130.1 1.1 fusion.22
  131.4 1.1 fusion.22
  140.1 2.6 %collective-permute-start.1 = (bf16[1,1,65536]{2,0,1:T(2,128)(2,1)S(1)}, bf16[1,1,65536]{2,0,1:T(2,128)(2,1)S(1)}, u32[]{:S(2)}, u32[]{:S(2)}) collective-permute-start(bf16[1,1,65536]{2,0,1:T(2,128)(2,1)S(1)} %reshape.77), channel_id=1, source_target_pairs={{0,28},{4,0},{8,4},{12,8},{16,12},{20,16},{24,20},{28,24},{1,29},{... | collective-permute-start | bytes 393224 | tf_op jit(solution)/shard_map/ppermute | solution.py:74
  142.8 5.1 %collective-permute-done = bf16[1,1,65536]{2,0,1:T(2,128)(2,1)S(1)} collective-permute-done((bf16[1,1,65536]{2,0,1:T(2,128)(2,1)S(1)}, bf16[1,1,65536]{2,0,1:T(2,128)(2,1)S(1)}, u32[]{:S(2)}, u32[]{:S(2)}) %collective-permute-start) | collective-permute-done | bytes 131104 | tf_op jit(solution)/shard_map/ppermute | solution.py:71
  148.5 2.8 %collective-permute-start.3 = (bf16[1,1,65536]{2,0,1:T(2,128)(2,1)S(1)}, bf16[1,1,65536]{2,0,1:T(2,128)(2,1)S(1)}, u32[]{:S(2)}, u32[]{:S(2)}) collective-permute-start(bf16[1,1,65536]{2,0,1:T(2,128)(2,1)S(1)} %collective-permute-done.1), channel_id=1, source_target_pairs={{0,28},{4,0},{8,4},{12,8},{16,12},{20,16},{24,20},{28,24},{1,29},{... | collective-permute-start | bytes 393224 | tf_op jit(solution)/shard_map/ppermute | solution.py:74
  151.3 5.0 %collective-permute-done.2 = bf16[1,1,65536]{2,0,1:T(2,128)(2,1)S(1)} collective-permute-done((bf16[1,1,65536]{2,0,1:T(2,128)(2,1)S(1)}, bf16[1,1,65536]{2,0,1:T(2,128)(2,1)S(1)}, u32[]{:S(2)}, u32[]{:S(2)}) %collective-permute-start.2) | collective-permute-done | bytes 131104 | tf_op jit(solution)/shard_map/ppermute | solution.py:71
  156.3 2.7 %collective-permute-start.5 = (bf16[1,1,65536]{2,0,1:T(2,128)(2,1)S(1)}, bf16[1,1,65536]{2,0,1:T(2,128)(2,1)S(1)}, u32[]{:S(2)}, u32[]{:S(2)}) collective-permute-start(bf16[1,1,65536]{2,0,1:T(2,128)(2,1)S(1)} %collective-permute-done.3), channel_id=1, source_target_pairs={{0,28},{4,0},{8,4},{12,8},{16,12},{20,16},{24,20},{28,24},{1,29},{... | collective-permute-start | bytes 393224 | tf_op jit(solution)/shard_map/ppermute | solution.py:74
  159.0 6.4 %collective-permute-done.4 = bf16[1,1,65536]{2,0,1:T(2,128)(2,1)S(1)} collective-permute-done((bf16[1,1,65536]{2,0,1:T(2,128)(2,1)S(1)}, bf16[1,1,65536]{2,0,1:T(2,128)(2,1)S(1)}, u32[]{:S(2)}, u32[]{:S(2)}) %collective-permute-start.4) | collective-permute-done | bytes 131104 | tf_op jit(solution)/shard_map/ppermute | solution.py:71
  165.4 4.4 %dynamic_update_slice.28 = bf16[8,1,65536]{2,0,1:T(8,128)(2,1)S(1)} dynamic-update-slice(bf16[8,1,65536]{2,0,1:T(8,128)(2,1)S(1)} %broadcast_in_dim.13, bf16[1,1,65536]{2,0,1:T(2,128)(2,1)S(1)} %reshape.77, s32[]{:T(128)S(6)} %select_n.55, s32[]{:T(128)} %constant.88.clone.1, s32[]{:T(128)} %constant.88.clone.1) | dynamic-update-slice | bytes 262148 | tf_op jit(solution)/shard_map/dynamic_update_slice | solution.py:66
  169.9 4.4 %dynamic_update_slice.29 = bf16[8,1,65536]{2,0,1:T(8,128)(2,1)S(1)} dynamic-update-slice(bf16[8,1,65536]{2,0,1:T(8,128)(2,1)S(1)} %dynamic_update_slice.28, bf16[1,1,65536]{2,0,1:T(2,128)(2,1)S(1)} %collective-permute-done, s32[]{:T(128)S(6)} %select_n.57, s32[]{:T(128)} %constant.88.clone.1, s32[]{:T(128)} %constant.88.clone.1) | dynamic-update-slice | bytes 262148 | tf_op jit(solution)/shard_map/dynamic_update_slice | solution.py:72
  174.3 4.4 %dynamic_update_slice.30 = bf16[8,1,65536]{2,0,1:T(8,128)(2,1)S(1)} dynamic-update-slice(bf16[8,1,65536]{2,0,1:T(8,128)(2,1)S(1)} %dynamic_update_slice.29, bf16[1,1,65536]{2,0,1:T(2,128)(2,1)S(1)} %collective-permute-done.1, s32[]{:T(128)S(6)} %select_n.59, s32[]{:T(128)} %constant.88.clone.1, s32[]{:T(128)} %constant.88.clone.1) | dynamic-update-slice | bytes 262148 | tf_op jit(solution)/shard_map/dynamic_update_slice | solution.py:77
  178.7 4.4 %dynamic_update_slice.31 = bf16[8,1,65536]{2,0,1:T(8,128)(2,1)S(1)} dynamic-update-slice(bf16[8,1,65536]{2,0,1:T(8,128)(2,1)S(1)} %dynamic_update_slice.30, bf16[1,1,65536]{2,0,1:T(2,128)(2,1)S(1)} %collective-permute-done.2, s32[]{:T(128)S(6)} %select_n.61, s32[]{:T(128)} %constant.88.clone.1, s32[]{:T(128)} %constant.88.clone.1) | dynamic-update-slice | bytes 262148 | tf_op jit(solution)/shard_map/dynamic_update_slice | solution.py:72
  183.1 4.4 %dynamic_update_slice.32 = bf16[8,1,65536]{2,0,1:T(8,128)(2,1)S(1)} dynamic-update-slice(bf16[8,1,65536]{2,0,1:T(8,128)(2,1)S(1)} %dynamic_update_slice.31, bf16[1,1,65536]{2,0,1:T(2,128)(2,1)S(1)} %collective-permute-done.3, s32[]{:T(128)S(6)} %select_n.63, s32[]{:T(128)} %constant.88.clone.1, s32[]{:T(128)} %constant.88.clone.1) | dynamic-update-slice | bytes 262148 | tf_op jit(solution)/shard_map/dynamic_update_slice | solution.py:77
  187.6 4.4 %dynamic_update_slice.33 = bf16[8,1,65536]{2,0,1:T(8,128)(2,1)S(1)} dynamic-update-slice(bf16[8,1,65536]{2,0,1:T(8,128)(2,1)S(1)} %dynamic_update_slice.32, bf16[1,1,65536]{2,0,1:T(2,128)(2,1)S(1)} %collective-permute-done.4, s32[]{:T(128)S(6)} %select_n.65, s32[]{:T(128)} %constant.88.clone.1, s32[]{:T(128)} %constant.88.clone.1) | dynamic-update-slice | bytes 262148 | tf_op jit(solution)/shard_map/dynamic_update_slice | solution.py:72
  192.0 4.4 %dynamic_update_slice.34 = bf16[8,1,65536]{2,0,1:T(8,128)(2,1)S(1)} dynamic-update-slice(bf16[8,1,65536]{2,0,1:T(8,128)(2,1)S(1)} %dynamic_update_slice.33, bf16[1,1,65536]{2,0,1:T(2,128)(2,1)S(1)} %collective-permute-done.5, s32[]{:T(128)S(6)} %select_n.67, s32[]{:T(128)} %constant.88.clone.1, s32[]{:T(128)} %constant.88.clone.1) | dynamic-update-slice | bytes 262148 | tf_op jit(solution)/shard_map/dynamic_update_slice | solution.py:77
  196.5 4.4 %dynamic_update_slice.35 = bf16[8,1,65536]{2,0,1:T(8,128)(2,1)S(1)} dynamic-update-slice(bf16[8,1,65536]{2,0,1:T(8,128)(2,1)S(1)} %dynamic_update_slice.34, bf16[1,1,65536]{2,0,1:T(2,128)(2,1)S(1)} %collective-permute-done.6, s32[]{:T(128)S(6)} %select_n.69, s32[]{:T(128)} %constant.88.clone.1, s32[]{:T(128)} %constant.88.clone.1) | dynamic-update-slice | bytes 262148 | tf_op jit(solution)/shard_map/dynamic_update_slice | solution.py:72
  (71 shorter events, 11.2 us)
Async XLA Ops:
  7.2 68.3 %all-reduce.4.cloned.1.call-start = ((), (), s32[]{:S(2)}) async-start(), calls=%async_computation | async-start | bytes 4194304
  10.3 0.9 copy-start.6
  10.3 1.2 copy-start.7
  10.3 65.2 %copy-start = (f32[65536]{0:T(1024)S(1)}, f32[65536]{0:T(1024)}, u32[]{:S(2)}) copy-start(f32[65536]{0:T(1024)} %param.13) | copy-start | bytes 786436
  10.3 65.2 %copy-start.4 = (f32[65536]{0:T(1024)S(1)}, f32[65536]{0:T(1024)}, u32[]{:S(2)}) copy-start(f32[65536]{0:T(1024)} %param.15) | copy-start | bytes 786436
  10.3 65.2 %copy-start.5 = (f32[65536]{0:T(1024)S(1)}, f32[65536]{0:T(1024)}, u32[]{:S(2)}) copy-start(f32[65536]{0:T(1024)} %param.14) | copy-start | bytes 786436
  76.6 62.4 %copy-start.1 = (f32[65536]{0:T(1024)}, f32[65536]{0:T(1024)S(1)}, u32[]{:S(2)}) copy-start(f32[65536]{0:T(1024)S(1)} %get-tuple-element.120) | copy-start | bytes 786436
  76.6 62.4 %copy-start.2 = (f32[65536]{0:T(1024)}, f32[65536]{0:T(1024)S(1)}, u32[]{:S(2)}) copy-start(f32[65536]{0:T(1024)S(1)} %get-tuple-element.121) | copy-start | bytes 786436
  140.1 7.8 %collective-permute-start = (bf16[1,1,65536]{2,0,1:T(2,128)(2,1)S(1)}, bf16[1,1,65536]{2,0,1:T(2,128)(2,1)S(1)}, u32[]{:S(2)}, u32[]{:S(2)}) collective-permute-start(bf16[1,1,65536]{2,0,1:T(2,128)(2,1)S(1)} %reshape.77), channel_id=1, source_target_pairs={{0,4},{4,8},{8,12},{12,16},{16,20},{20,24},{24,28},{28,0},{1,5},{5... | collective-permute-start | bytes 393224 | tf_op jit(solution)/shard_map/ppermute | solution.py:71
  140.1 8.4 %collective-permute-start.1 = (bf16[1,1,65536]{2,0,1:T(2,128)(2,1)S(1)}, bf16[1,1,65536]{2,0,1:T(2,128)(2,1)S(1)}, u32[]{:S(2)}, u32[]{:S(2)}) collective-permute-start(bf16[1,1,65536]{2,0,1:T(2,128)(2,1)S(1)} %reshape.77), channel_id=1, source_target_pairs={{0,28},{4,0},{8,4},{12,8},{16,12},{20,16},{24,20},{28,24},{1,29},{... | collective-permute-start | bytes 393224 | tf_op jit(solution)/shard_map/ppermute | solution.py:74
  147.9 8.4 %collective-permute-start.2 = (bf16[1,1,65536]{2,0,1:T(2,128)(2,1)S(1)}, bf16[1,1,65536]{2,0,1:T(2,128)(2,1)S(1)}, u32[]{:S(2)}, u32[]{:S(2)}) collective-permute-start(bf16[1,1,65536]{2,0,1:T(2,128)(2,1)S(1)} %collective-permute-done), channel_id=1, source_target_pairs={{0,4},{4,8},{8,12},{12,16},{16,20},{20,24},{24,28},{28,0},{1,5},{5... | collective-permute-start | bytes 393224 | tf_op jit(solution)/shard_map/ppermute | solution.py:71
  148.5 7.8 %collective-permute-start.3 = (bf16[1,1,65536]{2,0,1:T(2,128)(2,1)S(1)}, bf16[1,1,65536]{2,0,1:T(2,128)(2,1)S(1)}, u32[]{:S(2)}, u32[]{:S(2)}) collective-permute-start(bf16[1,1,65536]{2,0,1:T(2,128)(2,1)S(1)} %collective-permute-done.1), channel_id=1, source_target_pairs={{0,28},{4,0},{8,4},{12,8},{16,12},{20,16},{24,20},{28,24},{1,29},{... | collective-permute-start | bytes 393224 | tf_op jit(solution)/shard_map/ppermute | solution.py:74
  156.3 9.1 %collective-permute-start.4 = (bf16[1,1,65536]{2,0,1:T(2,128)(2,1)S(1)}, bf16[1,1,65536]{2,0,1:T(2,128)(2,1)S(1)}, u32[]{:S(2)}, u32[]{:S(2)}) collective-permute-start(bf16[1,1,65536]{2,0,1:T(2,128)(2,1)S(1)} %collective-permute-done.2), channel_id=1, source_target_pairs={{0,4},{4,8},{8,12},{12,16},{16,20},{20,24},{24,28},{28,0},{1,5},{5... | collective-permute-start | bytes 393224 | tf_op jit(solution)/shard_map/ppermute | solution.py:71
  156.3 35.7 %collective-permute-start.5 = (bf16[1,1,65536]{2,0,1:T(2,128)(2,1)S(1)}, bf16[1,1,65536]{2,0,1:T(2,128)(2,1)S(1)}, u32[]{:S(2)}, u32[]{:S(2)}) collective-permute-start(bf16[1,1,65536]{2,0,1:T(2,128)(2,1)S(1)} %collective-permute-done.3), channel_id=1, source_target_pairs={{0,28},{4,0},{8,4},{12,8},{16,12},{20,16},{24,20},{28,24},{1,29},{... | collective-permute-start | bytes 393224 | tf_op jit(solution)/shard_map/ppermute | solution.py:74
  165.3 31.1 %collective-permute-start.6 = (bf16[1,1,65536]{2,0,1:T(2,128)(2,1)S(1)}, bf16[1,1,65536]{2,0,1:T(2,128)(2,1)S(1)}, u32[]{:S(2)}, u32[]{:S(2)}) collective-permute-start(bf16[1,1,65536]{2,0,1:T(2,128)(2,1)S(1)} %collective-permute-done.4), channel_id=1, source_target_pairs={{0,4},{4,8},{8,12},{12,16},{16,20},{20,24},{24,28},{28,0},{1,5},{5... | collective-permute-start | bytes 393224 | tf_op jit(solution)/shard_map/ppermute | solution.py:71
  200.9 1.0 copy-start.3
Sparse Core Ops, SparseCore 0:
  11.2 64.1 all-reduce.3
